TPU v7x, 256 devices: a whole 4x4x8 slice. The times are simulated.
256 devices in a mesh: dp: 4 (over y), tensor: 16 (over z, core), owner: 4 (over x).
Axes of the slice: x: 4, y: 4, z: 8, core: 2. Of those that a mesh axis runs over, the one named last changes fastest.
Arguments:
- queries: bfloat16 [512, 8192], P(('dp', 'tensor'), 'owner'), may hold values from -360 to 360
- cached_key_rows: bfloat16 [512, 512, 8, 128], P(('dp', 'tensor'), None, 'owner'), may hold values from -6 to 6
- cached_value_rows: bfloat16 [512, 512, 8, 128], P(('dp', 'tensor'), None, 'owner'), may hold values from -6 to 6
- newest_key: bfloat16 [512, 8, 128], P(('dp', 'tensor'), 'owner'), may hold values from -6 to 6
- newest_value: bfloat16 [512, 8, 128], P(('dp', 'tensor'), 'owner'), may hold values from -6 to 6
- output_weight: bfloat16 [8, 1024, 8192], P('owner', 'tensor'), may hold values from -0.75 to 0.75
- adapter_down_weight: bfloat16 [128, 8, 1024, 64], P('owner', None, 'tensor'), may hold values from -0.5 to 0.5
- adapter_up_weight: bfloat16 [128, 64, 8192], P('owner', None, 'tensor'), may hold values from -0.75 to 0.75
- adapter_store_row: int32 [128], replicated, may hold values from 0 to 127, each once
- adapters_by_group: int32 [4, 16], P('dp'), may hold values from 0 to 127, as said below
- adapter_per_row: int32 [512], P('dp'), may hold values from 0 to 127, as said below
Outputs:
- output: bfloat16 [512, 8192], P('dp', ('tensor', 'owner'))
Inputs may be any that keep to these rules, and one draw needn't show every extreme that they name: `adapter_per_row`: the rows g * 128 to (g + 1) * 128 - 1 form dp group g; each row's adapter is one of its group's listed adapters, and each listed one is used by some row of the group. `adapters_by_group`: the 16 adapters of a group are distinct.
All inputs are finite; a program needn't handle non-finite values.
Results may differ from a plain program's by a relative error of at most 0.015.
Values may be sent and summed in bfloat16 or wider, within the bound.
No kernel may reach another device: no remote copies, remote signals or barrier semaphores. Data moves between devices by JAX's collectives and lax.ppermute only.
A program may use at most 128 MiB of HBM per device.

v0:
```python
import jax
import jax.numpy as jnp
from jax import lax
from jax.sharding import PartitionSpec as P

ADAPTER_SCALE = 2.0


def shards(
    queries,
    cached_key_rows,
    cached_value_rows,
    newest_key,
    newest_value,
    output_weight,
    adapter_down_weight,
    adapter_up_weight,
    adapter_store_row,
    adapters_by_group,
    adapter_per_row,
):
    owner_index = lax.axis_index("owner")
    row_count = queries.shape[0]
    local_heads = newest_key.shape[1]
    head_width = newest_key.shape[2]
    group_width = queries.shape[1] // local_heads
    query_heads = queries.reshape(row_count, local_heads, group_width // head_width, head_width)
    inverse_root = head_width ** (-0.5)
    scores = (
        jnp.einsum(
            "rkgh,rckh->rkgc", query_heads, cached_key_rows, preferred_element_type=jnp.float32
        )
        * inverse_root
    )
    fresh_score = (
        jnp.einsum("rkgh,rkh->rkg", query_heads, newest_key, preferred_element_type=jnp.float32)
        * inverse_root
    )
    overall = jnp.maximum(jnp.max(scores, axis=-1), fresh_score)
    weights_exp = jnp.exp(scores - overall[..., None])
    fresh_weight = jnp.exp(fresh_score - overall)
    denominator = jnp.sum(weights_exp, axis=-1) + fresh_weight
    mixed = jnp.einsum(
        "rkgc,rckh->rkgh", weights_exp, cached_value_rows, preferred_element_type=jnp.float32
    )
    mixed = mixed + fresh_weight[..., None] * newest_value.astype(jnp.float32)[:, :, None, :]
    mixed = (
        (mixed / denominator[..., None])
        .astype(jnp.bfloat16)
        .reshape(row_count, local_heads, group_width)
    )
    attention = lax.all_to_all(mixed, "tensor", split_axis=2, concat_axis=0, tiled=True)
    slot_ids = adapters_by_group[0]
    adapter_total = adapter_store_row.shape[0]
    matches = slot_ids[:, None] == jnp.arange(adapter_total, dtype=jnp.int32)[None, :]
    slot_home = jnp.sum(jnp.where(matches, adapter_store_row[None, :], 0), axis=1)
    store_count = adapter_down_weight.shape[0]
    slot_match = (adapter_per_row[:, None] == slot_ids[None, :]).astype(jnp.float32)
    position = slot_home - owner_index * store_count
    is_present = (position >= 0) & (position < store_count)
    clamped_index = jnp.clip(position, 0, store_count - 1)
    down_projected = jnp.where(
        is_present[:, None, None, None], adapter_down_weight[clamped_index], 0
    )
    up_projected = jnp.where(is_present[:, None, None], adapter_up_weight[clamped_index], 0)
    down_total, up_total = (
        lax.psum_scatter(down_projected, "owner", scatter_dimension=1, tiled=True).astype(
            jnp.float32
        ),
        lax.psum_scatter(up_projected, "owner", scatter_dimension=2, tiled=True).astype(
            jnp.float32
        ),
    )
    slot_down = down_total.astype(jnp.bfloat16)
    slot_up = up_total.astype(jnp.bfloat16)
    rank_slots = jnp.einsum(
        "rkf,skfn->rsn", attention, slot_down, preferred_element_type=jnp.float32
    )
    rank_part = jnp.sum(slot_match[:, :, None] * rank_slots, axis=1)
    rank_code = lax.psum(rank_part, ("tensor", "owner")).astype(jnp.bfloat16)
    update_slots = jnp.einsum("rn,snc->rsc", rank_code, slot_up, preferred_element_type=jnp.float32)
    adapter_delta = jnp.sum(slot_match[:, :, None] * update_slots, axis=1)
    partial_sum = jnp.einsum(
        "rkf,kfd->rd", attention, output_weight, preferred_element_type=jnp.float32
    )
    base_output = lax.psum_scatter(
        partial_sum, ("tensor", "owner"), scatter_dimension=1, tiled=True
    )
    return (base_output + ADAPTER_SCALE * adapter_delta).astype(jnp.bfloat16)


def solution(mesh):
    return jax.shard_map(
        shards,
        mesh=mesh,
        in_specs=(
            P(("dp", "tensor"), "owner"),
            P(("dp", "tensor"), None, "owner", None),
            P(("dp", "tensor"), None, "owner", None),
            P(("dp", "tensor"), "owner", None),
            P(("dp", "tensor"), "owner", None),
            P("owner", "tensor", None),
            P("owner", None, "tensor", None),
            P("owner", None, "tensor"),
            P(),
            P("dp", None),
            P("dp"),
        ),
        out_specs=P("dp", ("tensor", "owner")),
        check_vma=False,
    )
```

profile of v0, /device:TPU:8, one launch (start us, length us, event | category | flops | bytes accessed | tf_op | source)
XLA Modules:
  0.0 342.8 jit_solution(8786427746575031881)
XLA Ops:
  6.5 0.0 copy-start
  6.5 0.0 all-reduce.3.cloned.1.call-start
  6.5 1.0 select_reduce_fusion
  7.6 4.3 %gather_fusion = bf16[16,8,64,64]{3,2,1,0:T(8,128)(2,1)} fusion(bf16[32,8,64,64]{3,2,1,0:T(8,128)(2,1)} %param.17, s32[1024]{0:T(1024)S(1)} %pad_clamp_fusion), kind=kCustom, calls=%fused_computation | custom fusion | bytes 2097216 | tf_op jit(solution)/shard_map/gather | solution.py:63
  11.9 3.1 broadcast_select_fusion
  15.1 0.0 all-reduce.3.cloned.1.call-update
  15.1 0.0 reduce-scatter.8.cloned.1.call-start
  15.1 3.2 gather_fusion.1
  18.3 1.4 broadcast_select_fusion.1
  19.7 2.9 copy.60
  22.6 0.0 copy-start.2
  22.6 0.0 copy-start.1
  22.6 0.0 copy-start.6
  22.6 4.2 %reshape.104 = bf16[512,1024]{1,0:T(8,128)(2,1)} reshape(bf16[512,16,64]{2,1,0:T(8,128)(2,1)} %bitcast.44) | data formatting | bytes 2097152
  26.8 0.0 reduce-scatter.8.cloned.1.call-update
  26.8 0.0 reduce-scatter.6.cloned.1.call-start
  26.9 0.0 copy-done.2
  26.9 0.0 copy-start.5
  26.9 0.0 copy-done.1
  26.9 0.0 copy-done.6
  26.9 0.1 fusion.25
  27.0 2.4 fusion.34
  29.5 0.2 fusion.21
  29.7 0.0 copy-done.5
  29.8 0.5 fusion.16
  30.2 0.3 copy.54
  30.5 0.5 reshape.107
  31.1 16.3 %all_to_all.18 = bf16[16,2,512]{2,1,0:T(2,128)(2,1)S(1)} all-to-all(bf16[16,2,512]{2,1,0:T(2,128)(2,1)S(1)} %reshape.107), channel_id=1, replica_groups=mesh['dp'=4,'tensor'=16,'owner'=4] {'tensor'}, dimensions={0} | all-to-all | bytes 65536 | tf_op jit(solution)/shard_map/all_to_all | solution.py:52
  47.3 0.6 reshape.108
  48.0 0.4 copy.56
  48.4 0.0 copy-done
  48.4 2.7 convolution_bitcast_fusion
  51.0 0.0 copy-start.7
  51.0 0.0 copy-start.3
  51.0 0.0 copy-start.4
  51.1 0.0 reduce-scatter.6.cloned.1.call-update
  51.1 0.6 copy-done.7
  51.7 0.6 dynamic-slice
  53.0 0.0 copy-done.3
  53.0 0.0 copy-done.4
  53.0 0.1 compare_convert_fusion
  53.1 28.9 %all-reduce.3.cloned.1.call-done = bf16[16,8,64,64]{3,2,1,0:T(8,128)(2,1)} async-done(((bf16[16,8,64,64]{3,2,1,0:T(8,128)(2,1)}), bf16[16,8,64,64]{3,2,1,0:T(8,128)(2,1)}) %all-reduce.3.cloned.1.call-update) | async-done | bytes 1048592
  81.9 1.4 fusion.6
  83.3 249.7 %psum.7 = bf16[128,64]{0,1:T(8,128)(2,1)S(1)} all-reduce(f32[128,64]{0,1:T(8,128)S(1)} %fusion.6), channel_id=1, replica_groups=mesh['dp'=4,'tensor'=16,'owner'=4] {'tensor','owner'}, use_global_device_ids=true, to_apply=%region_6.7 | all-reduce | flops 8192 | bytes 49152 | tf_op jit(solution)/shard_map/psum | solution.py:80
  333.0 0.0 reduce-scatter.8.cloned.1.call-done
  333.0 1.3 reshape.105
  334.4 0.4 fusion.4
  334.8 0.0 reduce-scatter.6.cloned.1.call-done
  334.8 1.5 add_convert_fusion
  (6 shorter events, 0.1 us)
Async XLA Ops:
  6.5 41.8 %copy-start = (bf16[2,64,8192]{2,1,0:T(8,128)(2,1)S(1)}, bf16[2,64,8192]{2,1,0:T(8,128)(2,1)}, u32[]{:S(2)}) copy-start(bf16[2,64,8192]{2,1,0:T(8,128)(2,1)} %param.16) | copy-start | bytes 6291460
  6.5 75.4 %all-reduce.3.cloned.1.call-start = ((), (), s32[]{:S(2)}) async-start(), calls=%async_computation.5 | async-start | bytes 4194304
  15.1 317.9 %reduce-scatter.8.cloned.1.call-start = ((), (), s32[]{:S(2)}) async-start(), calls=%async_computation.4 | async-start | bytes 1310720
  22.6 4.2 %copy-start.2 = (bf16[8,2,128]{2,1,0:T(2,128)(2,1)S(1)}, bf16[8,2,128]{2,1,0:T(2,128)(2,1)}, u32[]{:S(2)}) copy-start(bf16[8,2,128]{2,1,0:T(2,128)(2,1)} %param.15) | copy-start | bytes 12292
  22.6 4.3 %copy-start.1 = (bf16[8,2048]{1,0:T(8,128)(2,1)S(1)}, bf16[8,2048]{1,0:T(8,128)(2,1)}, u32[]{:S(2)}) copy-start(bf16[8,2048]{1,0:T(8,128)(2,1)} %param.11) | copy-start | bytes 98308
  22.6 4.3 %copy-start.6 = (bf16[8,2,128]{2,1,0:T(2,128)(2,1)S(1)}, bf16[8,2,128]{2,1,0:T(2,128)(2,1)}, u32[]{:S(2)}) copy-start(bf16[8,2,128]{2,1,0:T(2,128)(2,1)} %param.14) | copy-start | bytes 12292
  26.8 308.0 %reduce-scatter.6.cloned.1.call-start = ((), (), s32[]{:S(2)}) async-start(), calls=%async_computation.3 | async-start | bytes 4259840 | tf_op jit(solution)/shard_map/reduce_scatter | solution.py:86
  26.9 2.9 copy-start.5
  51.0 0.7 copy-start.7
  51.0 1.9 copy-start.3
  51.0 1.9 copy-start.4
Sparse Core Ops, SparseCore 0:
  15.2 66.6 all-reduce.2
  84.6 25.9 reduce-scatter.7
  114.8 143.6 reduce-scatter.5
where the time goes:
time: 343 us
  blocking collectives  266 us (78%)
  waiting for transfers between devices  28.9 us (8%)
  local copies, waits for them, and re-layouts  19 us (6%)
  between operations  13.9 us (4%)
  matrix products  7.54 us (2%)
  other arithmetic  7.3 us (2%)
    psum x1, blocking collectives, shards(): rank_code = lax.psum(rank_part, ('tensor', 'owner')).astype(jnp.bfloat16)  250 us
    unnamed x5, waiting for transfers between devices  28.9 us
    all_to_all x1, blocking collectives, shards(): lax.all_to_all(mixed, 'tensor', split_axis=2, concat_axis=0, tiled=True)  16.3 us
    unnamed x22, local copies, waits for them, and re-layouts  10.8 us
  transfers between devices with their start and end apart: 3, of which 1 were waited for; matrix products, arithmetic and copies ran while one was open for 7% of the time, Pallas kernels for 0%

commit v1 on v0

--- a/solution.py
+++ b/solution.py
@@ -4,6 +4,12 @@
 from jax.sharding import PartitionSpec as P
 
 ADAPTER_SCALE = 2.0
+
+
+def form_the_plane(row_axis, xs, ax_name):
+    for w in (row_axis, ax_name):
+        xs = lax.psum(xs, w)
+    return xs
 
 
 def shards(
@@ -77,7 +83,7 @@
         "rkf,skfn->rsn", attention, slot_down, preferred_element_type=jnp.float32
     )
     rank_part = jnp.sum(slot_match[:, :, None] * rank_slots, axis=1)
-    rank_code = lax.psum(rank_part, ("tensor", "owner")).astype(jnp.bfloat16)
+    rank_code = form_the_plane("owner", rank_part, "tensor").astype(jnp.bfloat16)
     update_slots = jnp.einsum("rn,snc->rsc", rank_code, slot_up, preferred_element_type=jnp.float32)
     adapter_delta = jnp.sum(slot_match[:, :, None] * update_slots, axis=1)
     partial_sum = jnp.einsum(

time: 343 us -> 267 us (0.78)
  blocking collectives: 266 us -> 77.7 us
  waiting for transfers between devices: 28.9 us -> 141 us
    psum x1 -> x2, blocking collectives: 250 us -> 61.4 us  [form_the_plane(): xs = lax.psum(xs, w)]
    reduce_scatter x1, waiting for transfers between devices: 0.02 us -> 112 us  [shards(): lax.psum_scatter(partial_sum, ('tensor', 'owner'), scatter_dimension=1, t...]
  transfers between devices with their start and end apart: 3 -> 3, of which waited for: 1 -> 2; matrix products, arithmetic and copies ran while one was open for 7% -> 9% of each run, Pallas kernels for 0% -> 0%
where the time goes in v1:
time: 267 us; the launch traced here: 266 us
  waiting for transfers between devices  141 us (53%)
  blocking collectives  77.7 us (29%)
  local copies, waits for them, and re-layouts  19 us (7%)
  between operations  13.9 us (5%)
  matrix products  7.54 us (3%)
  other arithmetic  7.3 us (3%)
    reduce_scatter x1, waiting for transfers between devices, shards(): lax.psum_scatter(partial_sum, ('tensor', 'owner'), scatter_dimension=1, t...  112 us
    psum x2, blocking collectives, form_the_plane(): xs = lax.psum(xs, w)  61.4 us
    unnamed x5, waiting for transfers between devices  28.9 us
    all_to_all x1, blocking collectives, shards(): lax.all_to_all(mixed, 'tensor', split_axis=2, concat_axis=0, tiled=True)  16.3 us
    unnamed x22, local copies, waits for them, and re-layouts  10.8 us
  transfers between devices with their start and end apart: 3, of which 2 were waited for; matrix products, arithmetic and copies ran while one was open for 9% of the time, Pallas kernels for 0%

profile of v1, /device:TPU:8, one launch (start us, length us, event | category | flops | bytes accessed | tf_op | source)
XLA Modules:
  0.0 266.4 jit_solution(1649633559219911371)
XLA Ops:
  6.5 0.0 copy-start
  6.5 0.0 all-reduce.3.cloned.1.call-start
  6.5 1.0 select_reduce_fusion
  7.6 4.3 %gather_fusion = bf16[16,8,64,64]{3,2,1,0:T(8,128)(2,1)} fusion(bf16[32,8,64,64]{3,2,1,0:T(8,128)(2,1)} %param.17, s32[1024]{0:T(1024)S(1)} %pad_clamp_fusion), kind=kCustom, calls=%fused_computation | custom fusion | bytes 2097216 | tf_op jit(solution)/shard_map/gather | solution.py:69
  11.9 3.1 %broadcast_select_fusion = bf16[16,8,64,64]{3,2,1,0:T(8,128)(2,1)} fusion(bf16[16,8,64,64]{3,2,1,0:T(8,128)(2,1)} %gather_fusion, pred[16]{0:T(512)(128)(4,1)S(1)} %compare_and_fusion), kind=kLoop, calls=%fused_computation.7 | loop fusion | flops 524288 | bytes 2097168 | tf_op jit(solution)/shard_map/jit(_where)/select_n | solution.py:68
  15.1 0.0 all-reduce.3.cloned.1.call-update
  15.1 0.0 reduce-scatter.8.cloned.1.call-start
  15.1 3.2 %gather_fusion.1 = bf16[16,64,512]{2,1,0:T(8,128)(2,1)} fusion(bf16[32,64,512]{2,1,0:T(8,128)(2,1)} %param.18, s32[1024]{0:T(1024)S(1)} %pad_clamp_fusion), kind=kCustom, calls=%fused_computation.1 | custom fusion | bytes 2097216 | tf_op jit(solution)/shard_map/gather | solution.py:71
  18.3 1.4 broadcast_select_fusion.1
  19.7 2.9 %copy.60 = bf16[16,64,512]{1,0,2:T(8,128)(2,1)} copy(bf16[16,64,512]{2,1,0:T(8,128)(2,1)S(1)} %broadcast_select_fusion.1) | data formatting | bytes 2097152
  22.6 0.0 copy-start.2
  22.6 0.0 copy-start.1
  22.6 0.0 copy-start.6
  22.6 4.2 %reshape.104 = bf16[512,1024]{1,0:T(8,128)(2,1)} reshape(bf16[512,16,64]{2,1,0:T(8,128)(2,1)} %bitcast.44) | data formatting | bytes 2097152
  26.8 0.0 reduce-scatter.8.cloned.1.call-update
  26.8 0.0 reduce-scatter.6.cloned.1.call-start
  26.9 0.0 copy-done.2
  26.9 0.0 copy-start.5
  26.9 0.0 copy-done.1
  26.9 0.0 copy-done.6
  26.9 0.1 fusion.25
  27.0 2.4 fusion.34
  29.5 0.2 fusion.21
  29.7 0.0 copy-done.5
  29.8 0.5 fusion.16
  30.2 0.3 copy.54
  30.5 0.5 reshape.107
  31.1 16.3 %all_to_all.18 = bf16[16,2,512]{2,1,0:T(2,128)(2,1)S(1)} all-to-all(bf16[16,2,512]{2,1,0:T(2,128)(2,1)S(1)} %reshape.107), channel_id=1, replica_groups=mesh['dp'=4,'tensor'=16,'owner'=4] {'tensor'}, dimensions={0} | all-to-all | bytes 65536 | tf_op jit(solution)/shard_map/all_to_all | solution.py:58
  47.3 0.6 reshape.108
  48.0 0.4 copy.56
  48.4 0.0 copy-done
  48.4 2.7 %convolution_bitcast_fusion = f32[128,8192]{1,0:T(8,128)} fusion(bf16[2,64,8192]{2,1,0:T(8,128)(2,1)S(1)} %copy-done, bf16[8,2,16,64]{3,0,2,1:T(8,128)(2,1)S(1)} %copy.56), kind=kOutput, calls=%fused_computation.2 | convolution fusion | flops 268435456 | bytes 6324224 | tf_op jit(solution)/shard_map/rkf,kfd->rd/dot_general | solution.py:89
  51.0 0.0 copy-start.7
  51.0 0.0 copy-start.3
  51.0 0.0 copy-start.4
  51.1 0.0 reduce-scatter.6.cloned.1.call-update
  51.1 0.6 copy-done.7
  51.7 0.6 dynamic-slice
  53.0 0.0 copy-done.3
  53.0 0.0 copy-done.4
  53.0 0.1 compare_convert_fusion
  53.1 28.9 %all-reduce.3.cloned.1.call-done = bf16[16,8,64,64]{3,2,1,0:T(8,128)(2,1)} async-done(((bf16[16,8,64,64]{3,2,1,0:T(8,128)(2,1)}), bf16[16,8,64,64]{3,2,1,0:T(8,128)(2,1)}) %all-reduce.3.cloned.1.call-update) | async-done | bytes 1048592
  81.9 1.4 fusion.6
  83.3 15.2 %psum.14 = f32[128,64]{0,1:T(8,128)S(1)} all-reduce(f32[128,64]{0,1:T(8,128)S(1)} %fusion.6), channel_id=1, replica_groups=mesh['dp'=4,'tensor'=16,'owner'=4] {'owner'}, use_global_device_ids=true, to_apply=%region_6.7 | all-reduce | flops 8192 | bytes 65536 | tf_op jit(solution)/shard_map/psum | solution.py:11
  98.5 46.2 %psum.15 = bf16[128,64]{0,1:T(8,128)(2,1)S(1)} all-reduce(f32[128,64]{0,1:T(8,128)S(1)} %psum.14), channel_id=1, replica_groups=mesh['dp'=4,'tensor'=16,'owner'=4] {'tensor'}, use_global_device_ids=true, to_apply=%region_7.8 | all-reduce | flops 8192 | bytes 49152 | tf_op jit(solution)/shard_map/psum | solution.py:11
  144.8 0.0 reduce-scatter.8.cloned.1.call-done
  144.8 1.3 reshape.105
  146.1 0.4 fusion.4
  146.5 111.8 %reduce-scatter.6.cloned.1.call-done = f32[128,128]{1,0:T(8,128)} async-done(((f32[128,8192]{1,0:T(8,128)}), f32[128,128]{1,0:T(8,128)}) %reduce-scatter.6.cloned.1.call-update) | async-done | bytes 65552 | tf_op jit(solution)/shard_map/reduce_scatter | solution.py:92
  258.4 1.5 add_convert_fusion
  (6 shorter events, 0.1 us)
Async XLA Ops:
  6.5 41.8 %copy-start = (bf16[2,64,8192]{2,1,0:T(8,128)(2,1)S(1)}, bf16[2,64,8192]{2,1,0:T(8,128)(2,1)}, u32[]{:S(2)}) copy-start(bf16[2,64,8192]{2,1,0:T(8,128)(2,1)} %param.16) | copy-start | bytes 6291460
  6.5 75.4 %all-reduce.3.cloned.1.call-start = ((), (), s32[]{:S(2)}) async-start(), calls=%async_computation.5 | async-start | bytes 4194304
  15.1 129.7 %reduce-scatter.8.cloned.1.call-start = ((), (), s32[]{:S(2)}) async-start(), calls=%async_computation.4 | async-start | bytes 1310720
  22.6 4.2 %copy-start.2 = (bf16[8,2,128]{2,1,0:T(2,128)(2,1)S(1)}, bf16[8,2,128]{2,1,0:T(2,128)(2,1)}, u32[]{:S(2)}) copy-start(bf16[8,2,128]{2,1,0:T(2,128)(2,1)} %param.15) | copy-start | bytes 12292
  22.6 4.3 %copy-start.1 = (bf16[8,2048]{1,0:T(8,128)(2,1)S(1)}, bf16[8,2048]{1,0:T(8,128)(2,1)}, u32[]{:S(2)}) copy-start(bf16[8,2048]{1,0:T(8,128)(2,1)} %param.11) | copy-start | bytes 98308
  22.6 4.3 %copy-start.6 = (bf16[8,2,128]{2,1,0:T(2,128)(2,1)S(1)}, bf16[8,2,128]{2,1,0:T(2,128)(2,1)}, u32[]{:S(2)}) copy-start(bf16[8,2,128]{2,1,0:T(2,128)(2,1)} %param.14) | copy-start | bytes 12292
  26.8 231.6 %reduce-scatter.6.cloned.1.call-start = ((), (), s32[]{:S(2)}) async-start(), calls=%async_computation.3 | async-start | bytes 4259840 | tf_op jit(solution)/shard_map/reduce_scatter | solution.py:92
  26.9 2.9 %copy-start.5 = (bf16[8,512,2,128]{3,2,1,0:T(2,128)(2,1)S(1)}, bf16[8,512,2,128]{3,2,1,0:T(2,128)(2,1)}, u32[]{:S(2)}) copy-start(bf16[8,512,2,128]{3,2,1,0:T(2,128)(2,1)} %param.13) | copy-start | bytes 6291460
  51.0 0.7 copy-start.7
  51.0 1.9 copy-start.3
  51.0 1.9 copy-start.4
Sparse Core Ops, SparseCore 0:
  15.2 66.6 all-reduce.2
  84.6 25.8 reduce-scatter.7
  114.7 143.6 reduce-scatter.5
